TPU v7x, 32 devices: a whole 2x2x4 slice. The times are simulated.
32 devices in a mesh: mpo: 4 (over x, core), bond: 8 (over z, y).
Axes of the slice: x: 2, y: 2, z: 4, core: 2. Of those that a mesh axis runs over, the one named last changes fastest.
Arguments:
- environment: bfloat16 [4096, 40, 4096], P(None, 'mpo', 'bond'), may hold values from -60 to 60
- site_tensor: bfloat16 [4096, 4, 4096], P('bond'), may hold values from -0.09375 to 0.09375
- mpo_tensor: bfloat16 [40, 40, 4, 4], replicated, may hold values from -0.5 to 0.5
- sketch_site: bfloat16 [4096, 128], replicated, may hold values from -6 to 6
- sketch_expand: bfloat16 [128, 40, 4096], P('mpo'), may hold values from -60 to 60
- row_sectors: int32 [2, 4096, 4], P(None, 'bond'), may hold values from 0 to 5, as said below
- column_sectors: int32 [2, 128], replicated, may hold values from 0 to 5, as said below
Outputs:
- basis: bfloat16 [4096, 4, 128], P('bond')
- extended: float32 [128, 40, 128], P('bond', 'mpo')
Inputs may be any that keep to these rules, and one draw needn't show every extreme that they name: `row_sectors`: every joined row's label pair is (4, 0) or (5, 1); the rows labelled (5, 1) are one run of 64 consecutive joined rows (a, s) in the order a then s. `column_sectors`: every column's label pair is (4, 0) or (5, 1); exactly 16 columns are labelled (5, 1).
All inputs are finite; a program needn't handle non-finite values.
Results may differ from a plain program's by a relative error of at most 0.0064.
Values may be sent and summed in bfloat16 or wider, within the bound.
A program may use at most 128 MiB of HBM per device.

v0:
```python
import jax
import jax.numpy as jnp
from jax import lax
from jax.sharding import PartitionSpec as P

mixing = 0.5
shift_tolerance = 1e-06


def sector_mask(row_labels, column_labels):
    match = (row_labels[0][:, :, None] == column_labels[0][None, None, :]) & (
        row_labels[1][:, :, None] == column_labels[1][None, None, :]
    )
    return match.astype(jnp.float32)


def gram_of(left, right):
    column_count = left.shape[-1]
    return jnp.dot(
        left.reshape(-1, column_count).T,
        right.reshape(-1, column_count),
        precision=lax.Precision.HIGHEST,
        preferred_element_type=jnp.float32,
    )


def orthonormal(factor, values):
    column_count = values.shape[-1]
    solved = jax.scipy.linalg.solve_triangular(
        factor, values.reshape(-1, column_count).T, lower=True
    )
    return solved.T.reshape(values.shape).astype(jnp.bfloat16)


def body(
    environment, site_tensor, mpo_tensor, sketch_site, sketch_expand, row_sectors, column_sectors
):
    mpo_index = lax.axis_index("mpo")
    mpo_count = lax.axis_size("mpo")
    physical_width = environment.shape[1]
    local_rows = site_tensor.shape[0]
    physical = site_tensor.shape[1]
    column_count = column_sectors.shape[1]
    operator_rows = lax.dynamic_slice_in_dim(
        mpo_tensor, mpo_index * physical_width, physical_width, 0
    )
    sketched = jnp.einsum(
        "asb,kwb->wska", site_tensor, sketch_expand, preferred_element_type=jnp.float32
    ).astype(jnp.bfloat16)
    applied = jnp.einsum(
        "vwst,wtka->vska", mpo_tensor, sketched, preferred_element_type=jnp.float32
    ).astype(jnp.bfloat16)
    contracted = lax.all_to_all(applied, "mpo", split_axis=0, concat_axis=2, tiled=True)
    env_rows = environment
    expand_part = lax.psum_scatter(
        jnp.einsum("awc,wskc->ask", env_rows, contracted, preferred_element_type=jnp.float32),
        "bond",
        scatter_dimension=0,
        tiled=True,
    )
    mask_rows = sector_mask(row_sectors, column_sectors)
    share = local_rows // mpo_count
    offset = mpo_index * share
    expand_whole = lax.psum(expand_part, "mpo") * mask_rows
    site_whole = (
        jnp.dot(
            site_tensor.reshape(local_rows * physical, -1),
            sketch_site,
            preferred_element_type=jnp.float32,
        ).reshape(local_rows, physical, column_count)
        * mask_rows
    )
    part_site = lax.dynamic_slice_in_dim(site_whole, offset, share, 0)
    expansion_piece = lax.dynamic_slice_in_dim(expand_whole, offset, share, 0)
    square_site, square_expand = lax.psum(
        (jnp.sum(part_site * part_site), jnp.sum(expansion_piece * expansion_piece)),
        ("mpo", "bond"),
    )
    mix = mixing * jnp.sqrt((square_site + shift_tolerance) / (square_expand + shift_tolerance))
    combo_part = part_site + mix * expansion_piece
    gram_total = lax.psum(gram_of(combo_part, combo_part), ("mpo", "bond"))
    factor = jnp.linalg.cholesky(gram_total)
    basis_local = orthonormal(factor, site_whole + mix * expand_whole)
    flat_basis = basis_local.reshape(local_rows, physical * column_count)
    piece = lax.all_gather(basis_local, "bond", axis=0, tiled=True)
    env_rows = environment
    projected = jnp.einsum(
        "ax,awc->wxc",
        piece.reshape(piece.shape[0], -1),
        env_rows,
        preferred_element_type=jnp.float32,
    ).astype(jnp.bfloat16)
    couple_merged = jnp.einsum(
        "wxc,cy->wxy", projected, flat_basis, preferred_element_type=jnp.float32
    ).reshape(physical_width, physical, column_count, physical, column_count)
    boundary_share = jnp.einsum(
        "wvst,wsktl->kvl",
        operator_rows.astype(jnp.float32),
        couple_merged,
        precision=lax.Precision.HIGHEST,
    )
    reduced = lax.psum_scatter(boundary_share, "bond", scatter_dimension=0, tiled=True)
    extended = lax.psum_scatter(reduced, "mpo", scatter_dimension=1, tiled=True)
    return (basis_local, extended)


def solution(mesh):
    placed = (
        P(None, "mpo", "bond"),
        P("bond", None, None),
        P(),
        P(),
        P("mpo", None, None),
        P(None, "bond", None),
        P(),
    )
    return jax.shard_map(
        body,
        mesh=mesh,
        in_specs=placed,
        out_specs=(P("bond", None, None), P("bond", "mpo", None)),
        check_vma=False,
    )
```

profile of v0, /device:TPU:0, one launch (start us, length us, event | category | flops | bytes accessed | tf_op | source)
XLA Modules:
  0.0 739.9 jit_solution(15109001147891510651)
XLA Ops:
  7.2 0.0 copy-start
  7.2 0.0 copy-start.2
  7.2 0.0 reduce-scatter.4.cloned.1.call-start
  7.2 31.3 %fusion.4 = bf16[32,40,512,4]{2,1,3,0:T(8,128)(2,1)} fusion(bf16[512,4,4096]{2,1,0:T(4,128)(2,1)} %param.8, bf16[32,40,4096]{2,1,0:T(8,128)(2,1)} %param.11), kind=kOutput, calls=%fused_computation.4 | convolution fusion | flops 21474836480 | bytes 32505856 | tf_op jit(solution)/shard_map/asb,kwb->wska/dot_general | solution.py:47
  38.5 0.0 copy-done.2
  38.5 4.6 fusion.13
  43.1 2.7 copy.35
  45.8 63.4 %all_to_all.18 = bf16[40,4,32,512]{3,1,2,0:T(4,128)(2,1)S(1)} all-to-all(bf16[40,4,32,512]{3,1,2,0:T(4,128)(2,1)S(1)} %copy.35), channel_id=1, replica_groups=mesh['mpo'=4,'bond'=8] {'mpo'}, dimensions={0} | all-to-all | bytes 10485760 | tf_op jit(solution)/shard_map/all_to_all | solution.py:53
  109.2 1.7 copy.36
  110.9 0.6 copy.37
  111.6 0.0 copy-start.4
  111.6 0.0 copy-start.3
  111.6 27.7 %fusion.10 = f32[4096,4,128]{2,0,1:T(8,128)} fusion(bf16[10,4,128,512]{3,2,0,1:T(8,128)(2,1)S(1)} %bitcast.100, bf16[4096,10,512]{2,0,1:T(8,128)(2,1)} %param.7), kind=kOutput, calls=%fused_computation.11 | convolution fusion | flops 21474836480 | bytes 55574528 | tf_op jit(solution)/shard_map/awc,wskc->ask/dot_general | solution.py:56
  139.3 0.0 reduce-scatter.4.cloned.1.call-update
  139.3 0.0 all-reduce.4.cloned.1.call-start
  139.4 0.0 copy-done.4
  139.4 0.0 copy-done.3
  139.4 148.3 %reduce-scatter.4.cloned.1.call-done = f32[512,4,128]{2,0,1:T(8,128)} async-done(((f32[4096,4,128]{2,0,1:T(8,128)}), f32[512,4,128]{2,0,1:T(8,128)}) %reduce-scatter.4.cloned.1.call-update) | async-done | bytes 1048592 | tf_op jit(solution)/shard_map/reduce_scatter | solution.py:55
  287.7 0.0 all-reduce.4.cloned.1.call-update
  287.7 0.0 all-reduce.6.cloned.1.call-start
  287.8 0.0 copy-done
  287.8 30.4 %fusion.22 = f32[512,4,128]{2,0,1:T(8,128)S(1)} fusion(bf16[512,4,4096]{2,1,0:T(4,128)(2,1)} %param.8, bf16[4096,128]{1,0:T(8,128)(2,1)S(1)} %copy-done, s32[128]{0:T(128)S(1)} %get-tuple-element.13, s32[512,4]{0,1:T(4,128)S(1)} %get-tuple-element.11, s32[128]{0:T(128)S(1)} %get-tuple-element.12, s32[512,4]{0,1:T(4,128)S(1)} %get-tuple-element.10), kind=kOutput, calls=%fused_computation.18 | convolution fusion | flops 2148532224 | bytes 18891776 | tf_op jit(solution)/shard_map/dot_general | solution.py:66
  318.2 0.7 multiply_reduce_fusion.1
  318.9 6.6 all-reduce.4.cloned.1.call-done
  325.5 1.8 fusion.28
  327.2 0.7 multiply_reduce_fusion
  327.9 40.0 %all-reduce = (f32[]{:T(128)}, f32[]{:T(128)}) all-reduce(f32[]{:T(128)} %multiply_reduce_fusion.1, f32[]{:T(128)} %multiply_reduce_fusion), channel_id=1, replica_groups=mesh['mpo'=4,'bond'=8] {'mpo','bond'}, use_global_device_ids=true, to_apply=%region_1.0 | all-reduce | flops 2 | bytes 16 | tf_op jit(solution)/shard_map/psum | solution.py:75
  369.3 1.2 convolution_bitcast_fusion
  370.5 0.0 all-reduce.6.cloned.1.call-update
  370.6 0.2 all-gather.2.cloned.1.call-start
  370.8 119.7 %all-reduce.6.cloned.1.call-done = f32[128,128]{0,1:T(8,128)} async-done(((f32[128,128]{0,1:T(8,128)}), f32[128,128]{0,1:T(8,128)}) %all-reduce.6.cloned.1.call-update) | async-done | bytes 65552 | tf_op jit(solution)/shard_map/psum | solution.py:81
  490.5 0.9 copy.41
  491.4 0.9 fusion.41
  492.3 11.7 %cholesky.16 = f32[128,128]{1,0:T(8,128)S(1)} custom-call(f32[128,128]{1,0:T(8,128)S(1)} %fusion.41), custom_call_target="Cholesky" | custom-call | tf_op jit(solution)/shard_map/jit(cholesky)/cholesky | solution.py:82
  504.0 0.6 compare_reduce_fusion
  504.7 0.7 fusion.38
  505.4 9.8 %custom-call.7 = f32[1,128,128]{1,2,0:T(8,128)S(1)} custom-call(f32[1,128,128]{2,1,0:T(8,128)S(1)} %fusion.38), custom_call_target="InvertDiagBlocksLowerTriangular" | custom-call | tf_op jit(solution)/shard_map/jit(_solve_triangular)/triangular_solve | solution.py:29
  515.2 2.0 convolution_convert_fusion.1
  517.1 0.0 all-gather.2.cloned.1.call-update
  517.2 0.0 reduce-scatter.6.cloned.1.call-start
  517.3 75.9 %all-gather.2.cloned.1.call-done = bf16[4096,4,128]{0,2,1:T(8,128)(2,1)} async-done(((bf16[512,4,128]{0,2,1:T(8,128)(2,1)}), bf16[4096,4,128]{0,2,1:T(8,128)(2,1)}) %all-gather.2.cloned.1.call-update) | async-done | bytes 4194320 | tf_op jit(solution)/shard_map/all_gather | solution.py:85
  593.2 0.0 copy-start.1
  593.2 27.9 %convolution_convert_fusion = bf16[512,10,512]{2,0,1:T(8,128)(2,1)S(1)} fusion(bf16[4096,512,1]{0,1,2:T(8,128)(2,1)} %bitcast.101, bf16[4096,10,512]{2,0,1:T(8,128)(2,1)} %param.7), kind=kOutput, calls=%fused_computation.16 | convolution fusion | flops 21477457920 | bytes 51380224 | tf_op jit(solution)/shard_map/ax,awc->wxc/dot_general | solution.py:87
  621.1 0.0 copy-done.1
  621.1 2.9 fusion.29
  624.0 16.9 %fusion.19 = f32[128,40,128]{2,1,0:T(8,128)} fusion(f32[10,4,128,4,128]{4,2,3,1,0:T(8,128)S(1)} %fusion.29, bf16[40,40,4,4]{1,0,3,2:T(8,128)(2,1)S(1)} %copy.34, s32[]{:T(128)S(6)} %select_n.13), kind=kOutput, calls=%fused_computation.17 | convolution fusion | flops 1258291200 | bytes 13172740 | tf_op jit(solution)/shard_map/wvst,wsktl->kvl/dot_general | solution.py:96
  640.9 0.0 reduce-scatter.6.cloned.1.call-update
  640.9 0.0 reduce-scatter.8.cloned.1.call-start
  640.9 69.2 %reduce-scatter.6.cloned.1.call-done = f32[16,40,128]{2,1,0:T(8,128)} async-done(((f32[128,40,128]{2,1,0:T(8,128)}), f32[16,40,128]{2,1,0:T(8,128)}) %reduce-scatter.6.cloned.1.call-update) | async-done | bytes 327696 | tf_op jit(solution)/shard_map/reduce_scatter | solution.py:102
  710.2 1.7 copy.45
  711.9 0.0 reduce-scatter.8.cloned.1.call-update
  711.9 1.1 copy.46
  713.0 19.7 %reduce-scatter.8.cloned.1.call-done = f32[16,10,128]{2,0,1:T(8,128)} async-done(((f32[16,40,128]{2,0,1:T(8,128)}), f32[16,10,128]{2,0,1:T(8,128)}) %reduce-scatter.8.cloned.1.call-update) | async-done | bytes 81936 | tf_op jit(solution)/shard_map/reduce_scatter | solution.py:103
  (4 shorter events, 0.1 us)
Async XLA Ops:
  7.2 280.6 %copy-start = (bf16[4096,128]{1,0:T(8,128)(2,1)S(1)}, bf16[4096,128]{1,0:T(8,128)(2,1)}, u32[]{:S(2)}) copy-start(bf16[4096,128]{1,0:T(8,128)(2,1)} %param.10) | copy-start | bytes 3145732
  7.2 31.4 %copy-start.2 = (bf16[40,40,4,4]{1,3,2,0:T(4,128)(2,1)S(1)}, bf16[40,40,4,4]{1,3,2,0:T(4,128)(2,1)}, u32[]{:S(2)}) copy-start(bf16[40,40,4,4]{1,3,2,0:T(4,128)(2,1)} %param.9) | copy-start | bytes 153604
  7.2 280.5 %reduce-scatter.4.cloned.1.call-start = ((), (), s32[]{:S(2)}) async-start(), calls=%async_computation.4 | async-start | bytes 9437184 | tf_op jit(solution)/shard_map/reduce_scatter | solution.py:55
  111.6 27.8 %copy-start.4 = (s32[2,128]{1,0:T(2,128)S(1)}, s32[2,128]{1,0:T(2,128)}, u32[]{:S(2)}) copy-start(s32[2,128]{1,0:T(2,128)} %param.13) | copy-start | bytes 3076
  111.6 27.8 %copy-start.3 = (s32[2,512,4]{1,2,0:T(4,128)S(1)}, s32[2,512,4]{1,2,0:T(4,128)}, u32[]{:S(2)}) copy-start(s32[2,512,4]{1,2,0:T(4,128)} %param.12) | copy-start | bytes 49156
  139.3 186.1 %all-reduce.4.cloned.1.call-start = ((), (), s32[]{:S(2)}) async-start(), calls=%async_computation.5 | async-start | bytes 2097152 | tf_op jit(solution)/shard_map/psum | solution.py:64
  287.7 202.8 %all-reduce.6.cloned.1.call-start = ((), (), s32[]{:S(2)}) async-start(), calls=%async_computation.6 | async-start | bytes 131072 | tf_op jit(solution)/shard_map/psum | solution.py:81
  370.6 222.6 %all-gather.2.cloned.1.call-start = ((), (), s32[]{:S(2)}) async-start(), calls=%async_computation.7 | async-start | bytes 4718592 | tf_op jit(solution)/shard_map/all_gather | solution.py:85
  517.2 193.0 %reduce-scatter.6.cloned.1.call-start = ((), (), s32[]{:S(2)}) async-start(), calls=%async_computation.8 | async-start | bytes 2949120 | tf_op jit(solution)/shard_map/reduce_scatter | solution.py:102
  593.2 27.9 %copy-start.1 = (bf16[512,4,128]{0,2,1:T(8,128)(2,1)S(1)}, bf16[512,4,128]{0,2,1:T(8,128)(2,1)}, u32[]{:S(2)}) copy-start(bf16[512,4,128]{0,2,1:T(8,128)(2,1)} %convolution_convert_fusion.1) | copy-start | bytes 1572868
  640.9 91.8 %reduce-scatter.8.cloned.1.call-start = ((), (), s32[]{:S(2)}) async-start(), calls=%async_computation.9 | async-start | bytes 409600 | tf_op jit(solution)/shard_map/reduce_scatter | solution.py:103
Sparse Core Ops, SparseCore 0:
  139.5 148.2 reduce-scatter.3
  290.1 35.3 all-reduce.3
  370.7 119.7 all-reduce.5
  517.3 75.8 all-gather.1
  641.0 69.0 reduce-scatter.5
  713.1 19.5 reduce-scatter.7
where the time goes:
time: 749 us; the launch traced here: 740 us
  waiting for transfers between devices  439 us (59%)
  matrix products  145 us (19%)
  blocking collectives  103 us (14%)
  other arithmetic  26.8 us (4%)
  between operations  16.1 us (2%)
  local copies, waits for them, and re-layouts  8.83 us (1%)
    reduce_scatter x1, waiting for transfers between devices, body(): lax.psum_scatter(jnp.einsum('awc,wskc->ask', env_rows, contracted, prefer...  148 us
    psum x1, waiting for transfers between devices, body(): gram_total = lax.psum(gram_of(combo_part, combo_part), ('mpo', 'bond'))  120 us
    all_gather x1, waiting for transfers between devices, body(): piece = lax.all_gather(basis_local, 'bond', axis=0, tiled=True)  75.9 us
    reduce_scatter x1, waiting for transfers between devices, body(): lax.psum_scatter(boundary_share, 'bond', scatter_dimension=0, tiled=True)  69.2 us
    all_to_all x1, blocking collectives, body(): lax.all_to_all(applied, 'mpo', split_axis=0, concat_axis=2, tiled=True)  63.4 us
    psum x1, blocking collectives, body(): lax.psum((jnp.sum(part_site * part_site), jnp.sum(expansion_piece * expan...  40 us
    dot_general x1, matrix products, body(): jnp.einsum('asb,kwb->wska', site_tensor, sketch_expand, preferred_element...  31.3 us
    dot_general x1, matrix products, body(): jnp.dot(site_tensor.reshape(local_rows * physical, -1), sketch_site, pref...  30.4 us
  transfers between devices with their start and end apart: 6, of which 6 were waited for; matrix products, arithmetic and copies ran while one was open for 4% of the time, Pallas kernels for 0%

commit v1 on v0

--- a/solution.py
+++ b/solution.py
@@ -78,7 +78,12 @@
     )
     mix = mixing * jnp.sqrt((square_site + shift_tolerance) / (square_expand + shift_tolerance))
     combo_part = part_site + mix * expansion_piece
-    gram_total = lax.psum(gram_of(combo_part, combo_part), ("mpo", "bond"))
+
+    def balance_axis_part_for(vector, link_axis):
+        carry_out = lax.all_gather(vector, axis_name=link_axis).sum(axis=0)
+        return carry_out
+
+    gram_total = balance_axis_part_for(gram_of(combo_part, combo_part), ("mpo", "bond"))
     factor = jnp.linalg.cholesky(gram_total)
     basis_local = orthonormal(factor, site_whole + mix * expand_whole)
     flat_basis = basis_local.reshape(local_rows, physical * column_count)

time: 749 us -> 683 us (0.912)
  waiting for transfers between devices: 439 us -> 374 us
    psum x1 -> x0, waiting for transfers between devices: 120 us -> none  [body(): gram_total = lax.psum(gram_of(combo_part, combo_part), ('mpo', 'bond'))]
    all_gather x0 -> x1, waiting for transfers between devices: none -> 56.7 us  [balance_axis_part_for(): carry_out = lax.all_gather(vector, axis_name=link_axis).sum(axis=0)]
  transfers between devices with their start and end apart: 6 -> 6, of which waited for: 6 -> 6; matrix products, arithmetic and copies ran while one was open for 4% -> 5% of each run, Pallas kernels for 0% -> 0%
where the time goes in v1:
time: 683 us; the launch traced here: 675 us
  waiting for transfers between devices  374 us (55%)
  matrix products  145 us (21%)
  blocking collectives  103 us (15%)
  other arithmetic  27.7 us (4%)
  between operations  16.1 us (2%)
  local copies, waits for them, and re-layouts  7.99 us (1%)
    reduce_scatter x1, waiting for transfers between devices, body(): lax.psum_scatter(jnp.einsum('awc,wskc->ask', env_rows, contracted, prefer...  148 us
    all_gather x1, waiting for transfers between devices, body(): piece = lax.all_gather(basis_local, 'bond', axis=0, tiled=True)  73.5 us
    reduce_scatter x1, waiting for transfers between devices, body(): lax.psum_scatter(boundary_share, 'bond', scatter_dimension=0, tiled=True)  69.4 us
    all_to_all x1, blocking collectives, body(): lax.all_to_all(applied, 'mpo', split_axis=0, concat_axis=2, tiled=True)  63.4 us
    all_gather x1, waiting for transfers between devices, balance_axis_part_for(): carry_out = lax.all_gather(vector, axis_name=link_axis).sum(axis=0)  56.7 us
    psum x1, blocking collectives, body(): lax.psum((jnp.sum(part_site * part_site), jnp.sum(expansion_piece * expan...  40 us
    dot_general x1, matrix products, body(): jnp.einsum('asb,kwb->wska', site_tensor, sketch_expand, preferred_element...  31.3 us
    dot_general x1, matrix products, body(): jnp.dot(site_tensor.reshape(local_rows * physical, -1), sketch_site, pref...  30.4 us
  transfers between devices with their start and end apart: 6, of which 6 were waited for; matrix products, arithmetic and copies ran while one was open for 5% of the time, Pallas kernels for 0%

profile of v1, /device:TPU:0, one launch (start us, length us, event | category | flops | bytes accessed | tf_op | source)
XLA Modules:
  0.0 674.7 jit_solution(15912210380041272262)
XLA Ops:
  7.2 0.0 copy-start
  7.2 0.0 copy-start.2
  7.2 0.0 reduce-scatter.4.cloned.1.call-start
  7.2 31.3 %fusion.4 = bf16[32,40,512,4]{2,1,3,0:T(8,128)(2,1)} fusion(bf16[512,4,4096]{2,1,0:T(4,128)(2,1)} %param.8, bf16[32,40,4096]{2,1,0:T(8,128)(2,1)} %param.11), kind=kOutput, calls=%fused_computation.4 | convolution fusion | flops 21474836480 | bytes 32505856 | tf_op jit(solution)/shard_map/asb,kwb->wska/dot_general | solution.py:47
  38.5 0.0 copy-done.2
  38.5 4.6 fusion.13
  43.1 2.7 copy.33
  45.8 63.4 %all_to_all.18 = bf16[40,4,32,512]{3,1,2,0:T(4,128)(2,1)S(1)} all-to-all(bf16[40,4,32,512]{3,1,2,0:T(4,128)(2,1)S(1)} %copy.33), channel_id=1, replica_groups=mesh['mpo'=4,'bond'=8] {'mpo'}, dimensions={0} | all-to-all | bytes 10485760 | tf_op jit(solution)/shard_map/all_to_all | solution.py:53
  109.2 1.7 copy.34
  110.9 0.6 copy.35
  111.6 0.0 copy-start.4
  111.6 0.0 copy-start.3
  111.6 27.7 %fusion.10 = f32[4096,4,128]{2,0,1:T(8,128)} fusion(bf16[10,4,128,512]{3,2,0,1:T(8,128)(2,1)S(1)} %bitcast.101, bf16[4096,10,512]{2,0,1:T(8,128)(2,1)} %param.7), kind=kOutput, calls=%fused_computation.11 | convolution fusion | flops 21474836480 | bytes 55574528 | tf_op jit(solution)/shard_map/awc,wskc->ask/dot_general | solution.py:56
  139.3 0.0 reduce-scatter.4.cloned.1.call-update
  139.3 0.0 all-reduce.3.cloned.1.call-start
  139.4 0.0 copy-done.4
  139.4 0.0 copy-done.3
  139.4 148.3 %reduce-scatter.4.cloned.1.call-done = f32[512,4,128]{2,0,1:T(8,128)} async-done(((f32[4096,4,128]{2,0,1:T(8,128)}), f32[512,4,128]{2,0,1:T(8,128)}) %reduce-scatter.4.cloned.1.call-update) | async-done | bytes 1048592 | tf_op jit(solution)/shard_map/reduce_scatter | solution.py:55
  287.7 0.0 all-reduce.3.cloned.1.call-update
  287.7 0.0 all-gather.6.cloned.1.call-start
  287.8 0.0 copy-done
  287.8 30.4 %fusion.22 = f32[512,4,128]{2,0,1:T(8,128)S(1)} fusion(bf16[512,4,4096]{2,1,0:T(4,128)(2,1)} %param.8, bf16[4096,128]{1,0:T(8,128)(2,1)S(1)} %copy-done, s32[128]{0:T(128)S(1)} %get-tuple-element.13, s32[512,4]{0,1:T(4,128)S(1)} %get-tuple-element.11, s32[128]{0:T(128)S(1)} %get-tuple-element.12, s32[512,4]{0,1:T(4,128)S(1)} %get-tuple-element.10), kind=kOutput, calls=%fused_computation.18 | convolution fusion | flops 2148532224 | bytes 18891776 | tf_op jit(solution)/shard_map/dot_general | solution.py:66
  318.2 0.7 multiply_reduce_fusion.1
  318.9 6.6 all-reduce.3.cloned.1.call-done
  325.5 1.8 fusion.28
  327.2 0.7 multiply_reduce_fusion
  327.9 40.0 %all-reduce = (f32[]{:T(128)}, f32[]{:T(128)}) all-reduce(f32[]{:T(128)} %multiply_reduce_fusion.1, f32[]{:T(128)} %multiply_reduce_fusion), channel_id=1, replica_groups=mesh['mpo'=4,'bond'=8] {'mpo','bond'}, use_global_device_ids=true, to_apply=%region_1.0 | all-reduce | flops 2 | bytes 16 | tf_op jit(solution)/shard_map/psum | solution.py:75
  369.3 1.2 convolution_bitcast_fusion
  370.5 0.0 all-gather.6.cloned.1.call-update
  370.6 0.2 all-gather.4.cloned.1.call-start
  370.8 56.7 %all-gather.6.cloned.1.call-done = f32[4096,128]{1,0:T(8,128)} async-done(((f32[128,128]{1,0:T(8,128)}), f32[4096,128]{1,0:T(8,128)}) %all-gather.6.cloned.1.call-update) | async-done | bytes 2097168 | tf_op jit(solution)/shard_map/all_gather | solution.py:83
  427.5 1.7 reduce_sum.29
  429.2 0.1 copy.38
  429.3 11.7 %cholesky.16 = f32[128,128]{1,0:T(8,128)S(1)} custom-call(f32[128,128]{1,0:T(8,128)S(1)} %fusion.41), custom_call_target="Cholesky" | custom-call | tf_op jit(solution)/shard_map/jit(cholesky)/cholesky | solution.py:87
  441.0 0.6 compare_reduce_fusion
  441.7 0.7 fusion.38
  442.3 9.8 %custom-call.7 = f32[1,128,128]{1,2,0:T(8,128)S(1)} custom-call(f32[1,128,128]{2,1,0:T(8,128)S(1)} %fusion.38), custom_call_target="InvertDiagBlocksLowerTriangular" | custom-call | tf_op jit(solution)/shard_map/jit(_solve_triangular)/triangular_solve | solution.py:29
  452.1 2.0 convolution_convert_fusion.1
  454.1 0.0 all-gather.4.cloned.1.call-update
  454.1 0.0 reduce-scatter.6.cloned.1.call-start
  454.2 73.5 %all-gather.4.cloned.1.call-done = bf16[4096,4,128]{0,2,1:T(8,128)(2,1)} async-done(((bf16[512,4,128]{0,2,1:T(8,128)(2,1)}), bf16[4096,4,128]{0,2,1:T(8,128)(2,1)}) %all-gather.4.cloned.1.call-update) | async-done | bytes 4194320 | tf_op jit(solution)/shard_map/all_gather | solution.py:90
  527.8 0.0 copy-start.1
  527.8 27.9 %convolution_convert_fusion = bf16[512,10,512]{2,0,1:T(8,128)(2,1)S(1)} fusion(bf16[4096,512,1]{0,1,2:T(8,128)(2,1)} %bitcast.103, bf16[4096,10,512]{2,0,1:T(8,128)(2,1)} %param.7), kind=kOutput, calls=%fused_computation.16 | convolution fusion | flops 21477457920 | bytes 51380224 | tf_op jit(solution)/shard_map/ax,awc->wxc/dot_general | solution.py:92
  555.6 0.0 copy-done.1
  555.7 2.9 fusion.29
  558.6 16.9 %fusion.19 = f32[128,40,128]{2,1,0:T(8,128)} fusion(f32[10,4,128,4,128]{4,2,3,1,0:T(8,128)S(1)} %fusion.29, bf16[40,40,4,4]{1,0,3,2:T(8,128)(2,1)S(1)} %copy.32, s32[]{:T(128)S(6)} %select_n.13), kind=kOutput, calls=%fused_computation.17 | convolution fusion | flops 1258291200 | bytes 13172740 | tf_op jit(solution)/shard_map/wvst,wsktl->kvl/dot_general | solution.py:101
  575.4 0.0 reduce-scatter.6.cloned.1.call-update
  575.5 0.0 reduce-scatter.8.cloned.1.call-start
  575.5 69.4 %reduce-scatter.6.cloned.1.call-done = f32[16,40,128]{2,1,0:T(8,128)} async-done(((f32[128,40,128]{2,1,0:T(8,128)}), f32[16,40,128]{2,1,0:T(8,128)}) %reduce-scatter.6.cloned.1.call-update) | async-done | bytes 327696 | tf_op jit(solution)/shard_map/reduce_scatter | solution.py:107
  644.9 1.7 copy.42
  646.6 0.0 reduce-scatter.8.cloned.1.call-update
  646.7 1.1 copy.43
  647.7 19.7 %reduce-scatter.8.cloned.1.call-done = f32[16,10,128]{2,0,1:T(8,128)} async-done(((f32[16,40,128]{2,0,1:T(8,128)}), f32[16,10,128]{2,0,1:T(8,128)}) %reduce-scatter.8.cloned.1.call-update) | async-done | bytes 81936 | tf_op jit(solution)/shard_map/reduce_scatter | solution.py:108
  (5 shorter events, 0.1 us)
Async XLA Ops:
  7.2 280.6 %copy-start = (bf16[4096,128]{1,0:T(8,128)(2,1)S(1)}, bf16[4096,128]{1,0:T(8,128)(2,1)}, u32[]{:S(2)}) copy-start(bf16[4096,128]{1,0:T(8,128)(2,1)} %param.10) | copy-start | bytes 3145732
  7.2 31.4 %copy-start.2 = (bf16[40,40,4,4]{1,3,2,0:T(4,128)(2,1)S(1)}, bf16[40,40,4,4]{1,3,2,0:T(4,128)(2,1)}, u32[]{:S(2)}) copy-start(bf16[40,40,4,4]{1,3,2,0:T(4,128)(2,1)} %param.9) | copy-start | bytes 153604
  7.2 280.5 %reduce-scatter.4.cloned.1.call-start = ((), (), s32[]{:S(2)}) async-start(), calls=%async_computation.4 | async-start | bytes 9437184 | tf_op jit(solution)/shard_map/reduce_scatter | solution.py:55
  111.6 27.8 %copy-start.4 = (s32[2,128]{1,0:T(2,128)S(1)}, s32[2,128]{1,0:T(2,128)}, u32[]{:S(2)}) copy-start(s32[2,128]{1,0:T(2,128)} %param.13) | copy-start | bytes 3076
  111.6 27.8 %copy-start.3 = (s32[2,512,4]{1,2,0:T(4,128)S(1)}, s32[2,512,4]{1,2,0:T(4,128)}, u32[]{:S(2)}) copy-start(s32[2,512,4]{1,2,0:T(4,128)} %param.12) | copy-start | bytes 49156
  139.3 186.1 %all-reduce.3.cloned.1.call-start = ((), (), s32[]{:S(2)}) async-start(), calls=%async_computation.5 | async-start | bytes 2097152 | tf_op jit(solution)/shard_map/psum | solution.py:64
  287.7 139.7 %all-gather.6.cloned.1.call-start = ((), (), s32[]{:S(2)}) async-start(), calls=%async_computation.9 | async-start | bytes 2162688 | tf_op jit(solution)/shard_map/all_gather | solution.py:83
  370.6 157.2 %all-gather.4.cloned.1.call-start = ((), (), s32[]{:S(2)}) async-start(), calls=%async_computation.6 | async-start | bytes 4718592 | tf_op jit(solution)/shard_map/all_gather | solution.py:90
  454.1 190.8 %reduce-scatter.6.cloned.1.call-start = ((), (), s32[]{:S(2)}) async-start(), calls=%async_computation.7 | async-start | bytes 2949120 | tf_op jit(solution)/shard_map/reduce_scatter | solution.py:107
  527.8 27.9 %copy-start.1 = (bf16[512,4,128]{0,2,1:T(8,128)(2,1)S(1)}, bf16[512,4,128]{0,2,1:T(8,128)(2,1)}, u32[]{:S(2)}) copy-start(bf16[512,4,128]{0,2,1:T(8,128)(2,1)} %convolution_convert_fusion.1) | copy-start | bytes 1572868
  575.5 91.9 %reduce-scatter.8.cloned.1.call-start = ((), (), s32[]{:S(2)}) async-start(), calls=%async_computation.8 | async-start | bytes 409600 | tf_op jit(solution)/shard_map/reduce_scatter | solution.py:108
Sparse Core Ops, SparseCore 0:
  139.5 148.2 reduce-scatter.3
  290.1 35.3 all-reduce.2
  370.7 56.7 all-gather.5
  454.3 73.4 all-gather.3
  575.6 69.2 reduce-scatter.5
  647.8 19.5 reduce-scatter.7
